TPU v7x, 256 devices: a whole 4x4x8 slice. The times are simulated.
256 devices in a mesh: grp: 2 (over core), fsdp: 16 (over y, z_lo), tp: 8 (over x, z_hi).
Axes of the slice: x: 4, y: 4, z: 8 (z_hi: 2, z_lo: 4; z = z_hi * 4 + z_lo), core: 2. Of those that a mesh axis runs over, the one named last changes fastest.
Arguments:
- frames: bfloat16 [2, 4096, 8192], P('grp', 'fsdp'), may hold values from -6 to 6
- rewards: bfloat16 [4096], P('fsdp'), may hold values from -5 to 5
- actions: int32 [2, 4096], P('grp', 'fsdp'), may hold values from 0 to 17
- fractions: int32 [2, 4096, 32], P('grp', 'fsdp'), may hold values from 0 to 63
- episode_shard: int32 [4096, 1], P('fsdp'), may hold values from 0 to 15, as said below
- table: float32 [64], replicated, may hold values from 0.02 to 0.98
- norm_gain: float32 [8192], replicated, may hold values from 0.1 to 1.9
- torso_weight: bfloat16 [8192, 4096], P(('grp', 'fsdp'), 'tp'), may hold values from -0.0625 to 0.0625
- embed_weight: bfloat16 [64, 4096], P(None, 'tp'), may hold values from -0.75 to 0.75
- value_weight: bfloat16 [18, 4096], P(None, 'tp'), may hold values from -0.59765625 to 0.59765625
Outputs:
- torso_grad: float32 [8192, 4096], P(('grp', 'fsdp'), 'tp')
- refreshed_weight: bfloat16 [8192, 4096], P(('grp', 'fsdp', 'tp'))
Inputs may be any that keep to these rules, and one draw needn't show every extreme that they name: `episode_shard`: of the rows of one index of fsdp, at most 24 belong to one learner shard, and in every such block some learner shard gets exactly 24; every learner shard gets at least one row from every block.
All inputs are finite; a program needn't handle non-finite values.
Results may differ from a plain program's by a relative error of at most 0.0075.
Values may be sent and summed in bfloat16 or wider, within the bound.
No kernel may reach another device: no remote copies, remote signals or barrier semaphores. Data moves between devices by JAX's collectives and lax.ppermute only.
A program may use at most 64 MiB of HBM per device.

v0:
```python
import jax
import jax.numpy as jnp
from jax import lax
from jax.sharding import PartitionSpec as P

ACTIONS = 18
COSINES = 64
FRACS = 64


def shards(
    frames,
    rewards,
    actions,
    fractions,
    episode_shard,
    table,
    norm_gain,
    torso_weight,
    embed_weight,
    value_weight,
):
    shard_total = lax.axis_size("fsdp")
    destination = episode_shard[:, 0]
    rows_block = destination.shape[0]
    lanes = jnp.arange(shard_total, dtype=jnp.int32)
    onehot = (destination[:, None] == lanes[None, :]).astype(jnp.int32)
    counts = lax.psum(jnp.sum(onehot.astype(jnp.float32), axis=0), "fsdp")
    row_weight = jnp.dot(
        onehot.astype(jnp.float32), float(rows_block) / counts, precision=lax.Precision.HIGHEST
    )
    rows_data = frames[0]
    action_rows = actions[0]
    fraction_rows = fractions[0]
    values = rows_data.astype(jnp.float32)
    mean_square = jnp.mean(values * values, axis=-1, keepdims=True)
    normed = (values * lax.rsqrt(mean_square + 1e-05) * norm_gain).astype(jnp.bfloat16)
    columns = normed
    preact = jnp.dot(
        columns,
        lax.all_gather(torso_weight, ("grp", "fsdp"), axis=0, tiled=True),
        preferred_element_type=jnp.float32,
    )
    choose_mask = (action_rows[:, None] == jnp.arange(ACTIONS, dtype=jnp.int32)[None, :]).astype(
        jnp.bfloat16
    )
    picked = jnp.dot(choose_mask, value_weight, preferred_element_type=jnp.float32)
    weighted = (jax.nn.silu(preact) * picked).astype(jnp.bfloat16)
    cosine = jnp.cos(
        jnp.pi * jnp.arange(COSINES, dtype=jnp.float32)[None, :] * table[:, None]
    ).astype(jnp.bfloat16)
    embedding = jax.nn.relu(
        jnp.dot(cosine, embed_weight, preferred_element_type=jnp.float32)
    ).astype(jnp.bfloat16)
    table_values = lax.dot_general(
        weighted, embedding, (((1,), (1,)), ((), ())), preferred_element_type=jnp.float32
    )
    selector = (
        fraction_rows[:, :, None] == jnp.arange(FRACS, dtype=jnp.int32)[None, None, :]
    ).astype(jnp.float32)
    partial_quant = jnp.einsum(
        "mj,mtj->mt", table_values, selector, precision=lax.Precision.HIGHEST
    )
    group_index = lax.axis_index("grp")
    own_slot = jnp.arange(2, dtype=jnp.int32)[:, None, None] == group_index
    stacked = jnp.where(
        own_slot, partial_quant[None, :, :], jnp.zeros_like(partial_quant)[None, :, :]
    )
    summed = lax.psum(stacked, ("grp", "tp"))
    target_quant = summed[0]
    online_quant = summed[1]
    learner = (group_index == 1).astype(jnp.float32)
    levels = jnp.einsum("mtj,j->mt", selector, table, precision=lax.Precision.HIGHEST)
    target_value = rewards.astype(jnp.float32)[:, None] + 0.99 * target_quant
    errors = target_value[:, None, :] - online_quant[:, :, None]
    weight = jnp.abs(levels[:, :, None] - (errors < 0).astype(jnp.float32))
    grad_quant = -(learner * row_weight)[:, None] * jnp.sum(
        weight * jnp.clip(errors, -1.0, 1.0), axis=-1
    )
    grad_table = jnp.einsum("mi,mij->mj", grad_quant, selector, precision=lax.Precision.HIGHEST)
    grad_feature = jnp.dot(
        grad_table, embedding.astype(jnp.float32), precision=lax.Precision.HIGHEST
    )
    gate_value = jax.nn.sigmoid(preact)
    grad_preact = (grad_feature * picked * gate_value * (1.0 + preact * (1.0 - gate_value))).astype(
        jnp.bfloat16
    )
    columns = normed
    torso_grad = lax.psum_scatter(
        lax.dot_general(
            columns, grad_preact, (((0,), (0,)), ((), ())), preferred_element_type=jnp.float32
        ),
        ("grp", "fsdp"),
        scatter_dimension=0,
        tiled=True,
    )
    updated = (torso_weight.astype(jnp.float32) - 0.01 * torso_grad).astype(jnp.bfloat16)
    refreshed_weight = lax.all_to_all(updated, "tp", split_axis=0, concat_axis=1, tiled=True)
    return (torso_grad, refreshed_weight)


def solution(mesh):
    placed = (
        P("grp", "fsdp", None),
        P("fsdp"),
        P("grp", "fsdp"),
        P("grp", "fsdp", None),
        P("fsdp", None),
        P(),
        P(),
        P(("grp", "fsdp"), "tp"),
        P(None, "tp"),
        P(None, "tp"),
    )
    return jax.shard_map(
        shards,
        mesh=mesh,
        in_specs=placed,
        out_specs=(P(("grp", "fsdp"), "tp"), P(("grp", "fsdp", "tp"), None)),
        check_vma=False,
    )
```

profile of v0, /device:TPU:1, one launch (start us, length us, event | category | flops | bytes accessed | tf_op | source)
XLA Modules:
  0.0 676.3 jit_solution(3532035005112224799)
XLA Ops:
  7.2 0.0 copy-start
  7.2 0.0 copy-start.7
  7.2 0.0 copy-start.5
  7.2 0.0 copy-start.4
  7.2 0.0 copy-start.6
  7.2 0.0 copy-start.2
  7.2 0.0 all-gather.2.cloned.1.call-start
  7.3 0.7 all-gather.2.cloned.1.call-update
  8.0 0.0 all-reduce.2.cloned.1.call-start
  8.0 0.8 convert_reduce_fusion
  8.8 39.0 %psum.14 = f32[16]{0:T(128)S(1)} all-reduce(f32[16]{0:T(128)S(1)} %convert_reduce_fusion), channel_id=1, replica_groups=mesh['grp'=2,'fsdp'=16,'tp'=8] {'fsdp'}, use_global_device_ids=true, to_apply=%region_2.0 | all-reduce | flops 16 | bytes 128 | tf_op jit(solution)/shard_map/psum | solution.py:28
  47.8 0.0 copy-start.3
  47.8 3.2 fusion
  51.0 0.0 copy-done.7
  51.0 0.1 fusion.25
  51.1 0.0 copy-done
  51.1 0.0 copy-done.5
  51.1 0.3 fusion.12
  51.4 0.0 copy-done.4
  51.4 0.0 copy-done.6
  51.5 0.3 fusion.19
  51.7 0.0 copy-done.2
  51.7 3.8 fusion.15
  55.5 0.0 copy-start.8
  55.5 27.9 %all-gather.2.cloned.1.call-done = bf16[8192,512]{1,0:T(8,128)(2,1)} async-done(((bf16[256,512]{1,0:T(8,128)(2,1)}), bf16[8192,512]{1,0:T(8,128)(2,1)}) %all-gather.2.cloned.1.call-update) | async-done | bytes 8388624 | tf_op jit(solution)/shard_map/all_gather | solution.py:41
  83.4 0.0 copy-done.3
  83.4 7.0 %fusion.10 = f32[256,512]{1,0:T(8,128)S(1)} fusion(bf16[8192,512]{1,0:T(8,128)(2,1)} %all-gather.2.cloned.1.call-done, bf16[1,256,8192]{2,1,0:T(8,128)(2,1)} %param.10, f32[8192]{0:T(1024)S(1)} %copy-done.3, f32[256]{0:T(256)S(1)} %add_rsqrt_fusion), kind=kOutput, calls=%fused_computation.17 | convolution fusion | flops 2155872256 | bytes 13140992 | tf_op jit(solution)/shard_map/dot_general | solution.py:39
  90.5 0.3 fusion.18
  90.8 0.4 select_reduce_fusion.1
  91.1 0.7 broadcast_select_fusion
  91.8 0.0 all-reduce.2.cloned.1.call-update
  91.9 0.0 reduce-scatter.2.cloned.1.call-start
  91.9 0.0 copy-done.8
  91.9 2.8 copy.17
  94.8 172.4 %all-reduce.2.cloned.1.call-done = f32[2,256,32]{1,2,0:T(8,128)} async-done(((f32[2,256,32]{1,2,0:T(8,128)}), f32[2,256,32]{1,2,0:T(8,128)}) %all-reduce.2.cloned.1.call-update) | async-done | bytes 65552 | tf_op jit(solution)/shard_map/psum | solution.py:69
  267.1 0.8 slice_bitcast_fusion
  267.9 0.8 fusion.22
  268.7 0.3 fusion.14
  269.0 0.4 select_reduce_fusion
  269.4 0.5 fusion.7
  270.0 10.4 %fusion.8 = f32[8192,512]{1,0:T(8,128)} fusion(bf16[256,512]{1,0:T(8,128)(2,1)S(1)} %fusion.7, bf16[1,256,8192]{2,1,0:T(8,128)(2,1)} %param.10, f32[8192]{0:T(1024)S(1)} %copy-done.3, f32[256]{0:T(256)S(1)} %add_rsqrt_fusion), kind=kOutput, calls=%fused_computation.16 | convolution fusion | flops 2155872256 | bytes 21267456 | tf_op jit(solution)/shard_map/dot_general | solution.py:90
  280.4 0.0 copy-start.1
  280.4 0.0 reduce-scatter.2.cloned.1.call-update
  280.4 370.4 %reduce-scatter.2.cloned.1.call-done = f32[256,512]{1,0:T(8,128)} async-done(((f32[8192,512]{1,0:T(8,128)}), f32[256,512]{1,0:T(8,128)}) %reduce-scatter.2.cloned.1.call-update) | async-done | bytes 524304 | tf_op jit(solution)/shard_map/reduce_scatter | solution.py:89
  650.8 0.0 copy-done.1
  650.8 1.1 subtract_convert_fusion
  651.9 17.1 %all_to_all.19 = bf16[8,32,512]{2,1,0:T(8,128)(2,1)S(1)} all-to-all(bf16[8,32,512]{2,1,0:T(8,128)(2,1)S(1)} %bitcast.39), channel_id=1, replica_groups=mesh['grp'=2,'fsdp'=16,'tp'=8] {'tp'}, dimensions={0} | all-to-all | bytes 524288 | tf_op jit(solution)/shard_map/all_to_all | solution.py:98
  669.0 0.7 copy.31
  (6 shorter events, 0.0 us)
Async XLA Ops:
  7.2 44.0 %copy-start = (bf16[64,512]{1,0:T(8,128)(2,1)S(1)}, bf16[64,512]{1,0:T(8,128)(2,1)}, u32[]{:S(2)}) copy-start(bf16[64,512]{1,0:T(8,128)(2,1)} %param.18) | copy-start | bytes 196612
  7.2 43.8 %copy-start.7 = (s32[256,1]{0,1:T(1,128)S(1)}, s32[256,1]{0,1:T(1,128)}, u32[]{:S(2)}) copy-start(s32[256,1]{0,1:T(1,128)} %param.14) | copy-start | bytes 3076
  7.2 43.9 %copy-start.5 = (f32[64]{0:T(128)S(1)}, f32[64]{0:T(128)}, u32[]{:S(2)}) copy-start(f32[64]{0:T(128)} %param.15) | copy-start | bytes 772
  7.2 44.2 %copy-start.4 = (bf16[18,512]{1,0:T(8,128)(2,1)S(1)}, bf16[18,512]{1,0:T(8,128)(2,1)}, u32[]{:S(2)}) copy-start(bf16[18,512]{1,0:T(8,128)(2,1)} %param.19) | copy-start | bytes 55300
  7.2 44.2 %copy-start.6 = (s32[1,256]{1,0:T(1,128)S(1)}, s32[1,256]{1,0:T(1,128)}, u32[]{:S(2)}) copy-start(s32[1,256]{1,0:T(1,128)} %param.12) | copy-start | bytes 3076
  7.2 44.5 %copy-start.2 = (s32[1,256,32]{1,2,0:T(8,128)S(1)}, s32[1,256,32]{1,2,0:T(8,128)}, u32[]{:S(2)}) copy-start(s32[1,256,32]{1,2,0:T(8,128)} %param.13) | copy-start | bytes 98308
  7.2 76.2 %all-gather.2.cloned.1.call-start = ((), (), s32[]{:S(2)}) async-start(), calls=%async_computation.2 | async-start | bytes 8650752 | tf_op jit(solution)/shard_map/all_gather | solution.py:41
  8.0 259.2 %all-reduce.2.cloned.1.call-start = ((), (), s32[]{:S(2)}) async-start(), calls=%async_computation.3 | async-start | bytes 131072 | tf_op jit(solution)/shard_map/psum | solution.py:69
  47.8 35.6 %copy-start.3 = (f32[8192]{0:T(1024)S(1)}, f32[8192]{0:T(1024)}, u32[]{:S(2)}) copy-start(f32[8192]{0:T(1024)} %param.16) | copy-start | bytes 98308
  55.5 36.4 %copy-start.8 = (bf16[256]{0:T(256)(128)(2,1)S(1)}, bf16[256]{0:T(256)(128)(2,1)}, u32[]{:S(2)}) copy-start(bf16[256]{0:T(256)(128)(2,1)} %param.11) | copy-start | bytes 1540
  91.9 558.9 %reduce-scatter.2.cloned.1.call-start = ((), (), s32[]{:S(2)}) async-start(), calls=%async_computation.4 | async-start | bytes 17301504 | tf_op jit(solution)/shard_map/reduce_scatter | solution.py:89
  280.4 370.4 %copy-start.1 = (bf16[256,512]{1,0:T(8,128)(2,1)S(1)}, bf16[256,512]{1,0:T(8,128)(2,1)}, u32[]{:S(2)}) copy-start(bf16[256,512]{1,0:T(8,128)(2,1)} %param.17) | copy-start | bytes 786436
Sparse Core Ops, SparseCore 0:
  9.9 73.4 all-gather.1
  92.0 175.1 all-reduce.1
  280.5 370.1 reduce-scatter.1
where the time goes:
time: 677 us; the launch traced here: 676 us
  waiting for transfers between devices  571 us (84%)
  blocking collectives  56.1 us (8%)
  matrix products  22.7 us (3%)
  between operations  13.9 us (2%)
  other arithmetic  7.65 us (1%)
    reduce_scatter x1, waiting for transfers between devices, shards(): lax.psum_scatter(lax.dot_general(columns, grad_preact, (((0,), (0,)), (()...  370 us
    psum x1, waiting for transfers between devices, shards(): summed = lax.psum(stacked, ('grp', 'tp'))  172 us
    psum x1, blocking collectives, shards(): counts = lax.psum(jnp.sum(onehot.astype(jnp.float32), axis=0), 'fsdp')  39 us
    all_gather x1, waiting for transfers between devices, shards(): lax.all_gather(torso_weight, ('grp', 'fsdp'), axis=0, tiled=True)  27.9 us
    all_to_all x1, blocking collectives, shards(): lax.all_to_all(updated, 'tp', split_axis=0, concat_axis=1, tiled=True)  17.1 us
  transfers between devices with their start and end apart: 3, of which 3 were waited for; matrix products, arithmetic and copies ran while one was open for 2% of the time, Pallas kernels for 0%

commit v1 on v0

--- a/solution.py
+++ b/solution.py
@@ -66,7 +66,7 @@
     stacked = jnp.where(
         own_slot, partial_quant[None, :, :], jnp.zeros_like(partial_quant)[None, :, :]
     )
-    summed = lax.psum(stacked, ("grp", "tp"))
+    summed = lax.psum(lax.psum(stacked, "tp"), "grp")
     target_quant = summed[0]
     online_quant = summed[1]
     learner = (group_index == 1).astype(jnp.float32)

time: 677 us -> 632 us (0.934)
  waiting for transfers between devices: 571 us -> 527 us
    psum x1 -> x2, waiting for transfers between devices: 172 us -> 127 us  [shards(): summed = lax.psum(lax.psum(stacked, 'tp'), 'grp')]
  transfers between devices with their start and end apart: 3 -> 4, of which waited for: 3 -> 4; matrix products, arithmetic and copies ran while one was open for 2% -> 2% of each run, Pallas kernels for 0% -> 0%
where the time goes in v1:
time: 632 us
  waiting for transfers between devices  527 us (83%)
  blocking collectives  55.9 us (9%)
  matrix products  22.7 us (4%)
  between operations  13.9 us (2%)
  other arithmetic  7.65 us (1%)
    reduce_scatter x1, waiting for transfers between devices, shards(): lax.psum_scatter(lax.dot_general(columns, grad_preact, (((0,), (0,)), (()...  371 us
    psum x2, waiting for transfers between devices, shards(): summed = lax.psum(lax.psum(stacked, 'tp'), 'grp')  127 us
    psum x1, blocking collectives, shards(): counts = lax.psum(jnp.sum(onehot.astype(jnp.float32), axis=0), 'fsdp')  39 us
    all_gather x1, waiting for transfers between devices, shards(): lax.all_gather(torso_weight, ('grp', 'fsdp'), axis=0, tiled=True)  27.9 us
    all_to_all x1, blocking collectives, shards(): lax.all_to_all(updated, 'tp', split_axis=0, concat_axis=1, tiled=True)  16.8 us
  transfers between devices with their start and end apart: 4, of which 4 were waited for; matrix products, arithmetic and copies ran while one was open for 2% of the time, Pallas kernels for 0%

profile of v1, /device:TPU:1, one launch (start us, length us, event | category | flops | bytes accessed | tf_op | source)
XLA Modules:
  0.0 631.9 jit_solution(6170733771334951054)
XLA Ops:
  7.2 0.0 copy-start
  7.2 0.0 copy-start.5
  7.2 0.0 copy-start.4
  7.2 0.0 copy-start.6
  7.2 0.0 copy-start.2
  7.2 0.0 all-gather.2.cloned.1.call-start
  7.3 0.7 all-gather.2.cloned.1.call-update
  8.0 0.0 all-reduce.3.cloned.1.call-start
  8.0 0.8 convert_reduce_fusion
  8.8 39.0 %psum.21 = f32[16]{0:T(128)S(1)} all-reduce(f32[16]{0:T(128)S(1)} %convert_reduce_fusion), channel_id=1, replica_groups=mesh['grp'=2,'fsdp'=16,'tp'=8] {'fsdp'}, use_global_device_ids=true, to_apply=%region_2.0 | all-reduce | flops 16 | bytes 128 | tf_op jit(solution)/shard_map/psum | solution.py:28
  47.9 0.0 copy-start.3
  47.9 3.2 fusion
  51.0 0.0 copy-done
  51.0 0.0 copy-done.5
  51.0 0.3 fusion.12
  51.4 0.0 copy-done.4
  51.4 0.0 copy-done.6
  51.4 0.3 fusion.19
  51.6 0.0 copy-done.2
  51.7 3.8 fusion.15
  55.4 0.0 copy-start.7
  55.4 0.0 copy-start.8
  55.4 27.9 %all-gather.2.cloned.1.call-done = bf16[8192,512]{1,0:T(8,128)(2,1)} async-done(((bf16[256,512]{1,0:T(8,128)(2,1)}), bf16[8192,512]{1,0:T(8,128)(2,1)}) %all-gather.2.cloned.1.call-update) | async-done | bytes 8388624 | tf_op jit(solution)/shard_map/all_gather | solution.py:41
  83.4 0.0 copy-done.3
  83.4 7.0 %fusion.10 = f32[256,512]{1,0:T(8,128)S(1)} fusion(bf16[8192,512]{1,0:T(8,128)(2,1)} %all-gather.2.cloned.1.call-done, bf16[1,256,8192]{2,1,0:T(8,128)(2,1)} %param.10, f32[8192]{0:T(1024)S(1)} %copy-done.3, f32[256]{0:T(256)S(1)} %add_rsqrt_fusion), kind=kOutput, calls=%fused_computation.17 | convolution fusion | flops 2155872256 | bytes 13140992 | tf_op jit(solution)/shard_map/dot_general | solution.py:39
  90.4 0.3 fusion.18
  90.7 0.4 select_reduce_fusion.1
  91.1 0.7 broadcast_select_fusion
  91.8 0.0 all-reduce.3.cloned.1.call-update
  91.8 0.0 all-reduce.5.cloned.1.call-start
  91.8 0.0 copy-done.7
  91.9 0.1 fusion.25
  92.0 98.3 %all-reduce.3.cloned.1.call-done = f32[2,256,32]{1,2,0:T(8,128)} async-done(((f32[2,256,32]{1,2,0:T(8,128)}), f32[2,256,32]{1,2,0:T(8,128)}) %all-reduce.3.cloned.1.call-update) | async-done | bytes 65552 | tf_op jit(solution)/shard_map/psum | solution.py:69
  190.3 0.0 all-reduce.5.cloned.1.call-update
  190.3 0.0 reduce-scatter.2.cloned.1.call-start
  190.4 0.0 copy-done.8
  190.4 2.8 copy.17
  193.3 29.2 %all-reduce.5.cloned.1.call-done = f32[2,256,32]{1,2,0:T(8,128)} async-done(((f32[2,256,32]{1,2,0:T(8,128)}), f32[2,256,32]{1,2,0:T(8,128)}) %all-reduce.5.cloned.1.call-update) | async-done | bytes 65552 | tf_op jit(solution)/shard_map/psum | solution.py:69
  222.4 0.8 slice_bitcast_fusion
  223.2 0.8 fusion.22
  223.9 0.3 fusion.14
  224.3 0.4 select_reduce_fusion
  224.7 0.5 fusion.7
  225.2 10.4 %fusion.8 = f32[8192,512]{1,0:T(8,128)} fusion(bf16[256,512]{1,0:T(8,128)(2,1)S(1)} %fusion.7, bf16[1,256,8192]{2,1,0:T(8,128)(2,1)} %param.10, f32[8192]{0:T(1024)S(1)} %copy-done.3, f32[256]{0:T(256)S(1)} %add_rsqrt_fusion), kind=kOutput, calls=%fused_computation.16 | convolution fusion | flops 2155872256 | bytes 21267456 | tf_op jit(solution)/shard_map/dot_general | solution.py:90
  235.6 0.0 copy-start.1
  235.6 0.0 reduce-scatter.2.cloned.1.call-update
  235.7 371.0 %reduce-scatter.2.cloned.1.call-done = f32[256,512]{1,0:T(8,128)} async-done(((f32[8192,512]{1,0:T(8,128)}), f32[256,512]{1,0:T(8,128)}) %reduce-scatter.2.cloned.1.call-update) | async-done | bytes 524304 | tf_op jit(solution)/shard_map/reduce_scatter | solution.py:89
  606.7 0.0 copy-done.1
  606.7 1.1 subtract_convert_fusion
  607.8 16.8 %all_to_all.19 = bf16[8,32,512]{2,1,0:T(8,128)(2,1)S(1)} all-to-all(bf16[8,32,512]{2,1,0:T(8,128)(2,1)S(1)} %bitcast.39), channel_id=1, replica_groups=mesh['grp'=2,'fsdp'=16,'tp'=8] {'tp'}, dimensions={0} | all-to-all | bytes 524288 | tf_op jit(solution)/shard_map/all_to_all | solution.py:98
  624.6 0.7 copy.31
  (6 shorter events, 0.0 us)
Async XLA Ops:
  7.2 43.9 %copy-start = (bf16[64,512]{1,0:T(8,128)(2,1)S(1)}, bf16[64,512]{1,0:T(8,128)(2,1)}, u32[]{:S(2)}) copy-start(bf16[64,512]{1,0:T(8,128)(2,1)} %param.18) | copy-start | bytes 196612
  7.2 43.9 %copy-start.5 = (f32[64]{0:T(128)S(1)}, f32[64]{0:T(128)}, u32[]{:S(2)}) copy-start(f32[64]{0:T(128)} %param.15) | copy-start | bytes 772
  7.2 44.2 %copy-start.4 = (bf16[18,512]{1,0:T(8,128)(2,1)S(1)}, bf16[18,512]{1,0:T(8,128)(2,1)}, u32[]{:S(2)}) copy-start(bf16[18,512]{1,0:T(8,128)(2,1)} %param.19) | copy-start | bytes 55300
  7.2 44.2 %copy-start.6 = (s32[1,256]{1,0:T(1,128)S(1)}, s32[1,256]{1,0:T(1,128)}, u32[]{:S(2)}) copy-start(s32[1,256]{1,0:T(1,128)} %param.12) | copy-start | bytes 3076
  7.2 44.4 %copy-start.2 = (s32[1,256,32]{1,2,0:T(8,128)S(1)}, s32[1,256,32]{1,2,0:T(8,128)}, u32[]{:S(2)}) copy-start(s32[1,256,32]{1,2,0:T(8,128)} %param.13) | copy-start | bytes 98308
  7.2 76.2 %all-gather.2.cloned.1.call-start = ((), (), s32[]{:S(2)}) async-start(), calls=%async_computation.2 | async-start | bytes 8650752 | tf_op jit(solution)/shard_map/all_gather | solution.py:41
  8.0 182.4 %all-reduce.3.cloned.1.call-start = ((), (), s32[]{:S(2)}) async-start(), calls=%async_computation.3 | async-start | bytes 131072 | tf_op jit(solution)/shard_map/psum | solution.py:69
  47.9 35.5 %copy-start.3 = (f32[8192]{0:T(1024)S(1)}, f32[8192]{0:T(1024)}, u32[]{:S(2)}) copy-start(f32[8192]{0:T(1024)} %param.16) | copy-start | bytes 98308
  55.4 36.4 %copy-start.7 = (s32[256,1]{0,1:T(1,128)S(1)}, s32[256,1]{0,1:T(1,128)}, u32[]{:S(2)}) copy-start(s32[256,1]{0,1:T(1,128)} %param.14) | copy-start | bytes 3076
  55.4 135.0 %copy-start.8 = (bf16[256]{0:T(256)(128)(2,1)S(1)}, bf16[256]{0:T(256)(128)(2,1)}, u32[]{:S(2)}) copy-start(bf16[256]{0:T(256)(128)(2,1)} %param.11) | copy-start | bytes 1540
  91.8 130.6 %all-reduce.5.cloned.1.call-start = ((), (), s32[]{:S(2)}) async-start(), calls=%async_computation.4 | async-start | bytes 131072 | tf_op jit(solution)/shard_map/psum | solution.py:69
  190.3 416.3 %reduce-scatter.2.cloned.1.call-start = ((), (), s32[]{:S(2)}) async-start(), calls=%async_computation.5 | async-start | bytes 17301504 | tf_op jit(solution)/shard_map/reduce_scatter | solution.py:89
  235.6 371.0 %copy-start.1 = (bf16[256,512]{1,0:T(8,128)(2,1)S(1)}, bf16[256,512]{1,0:T(8,128)(2,1)}, u32[]{:S(2)}) copy-start(bf16[256,512]{1,0:T(8,128)(2,1)} %param.17) | copy-start | bytes 786436
Sparse Core Ops, SparseCore 0:
  9.9 73.4 all-gather.1
  91.9 98.3 all-reduce.2
  193.0 29.3 all-reduce.4
  235.8 370.8 reduce-scatter.1
